TPU v7x, 256 devices: a whole 4x4x8 slice. The times are simulated.
256 devices in a mesh: pulse: 8 (over y, core), tile: 32 (over x, z).
Axes of the slice: x: 4, y: 4, z: 8, core: 2. Of those that a mesh axis runs over, the one named last changes fastest.
Arguments:
- echoes: bfloat16 [512, 2, 2, 16384], P(('pulse', 'tile')), may hold values from -6 to 6
- pulse_slope: bfloat16 [512, 2], P(('pulse', 'tile')), may hold values from -0.023925781 to 0.023925781
- pulse_shift: bfloat16 [512, 2], P(('pulse', 'tile')), may hold values from -3.140625 to 3.140625
- footprint: int32 [8, 32, 32], P('pulse'), may hold values from -1 to 63, as said below
- band_start: int32 [1024], P('tile'), may hold values from 0 to 13216
- row_phase: float32 [1024], P('tile'), may hold values from -1 to 1
Outputs:
- formed_image: float32 [2, 1024, 4096], P(None, 'tile', 'pulse')
Inputs may be any that keep to these rules, and one draw needn't show every extreme that they name: footprint[g, t] lists in rising order the numbers of group g's blocks whose echoes reach row strip t, then -1 to the end. It names at most one block of each run of 2 numbers that starts at a multiple of 2. In every group some list has 32 entries.
All inputs are finite; a program needn't handle non-finite values.
Results may differ from a plain program's by a relative error of at most 0.0039.
Values may be sent and summed in bfloat16 or wider, within the bound.
No kernel may reach another device: no remote copies, remote signals or barrier semaphores. Data moves between devices by JAX's collectives and lax.ppermute only.
A program may use at most 64 MiB of HBM per device.

v0:
```python
import jax
import jax.numpy as jnp
from jax import lax
from jax.sharding import PartitionSpec as P

NCOL = 4096
PB = 2
ITERS = 2
step_size = 0.5
tv_weight = 0.4
floor_square = 0.25


def padded_2(value, sides, width):
    for axis, dim in sides:
        size, length = (lax.axis_size(axis), value.shape[dim])
        up = [(i, (i + 1) % size) for i in range(size - 1)]
        down = [(j, i) for i, j in up]
        last = lax.slice_in_dim(value, length - width, length, axis=dim)
        leading = lax.slice_in_dim(value, 0, width, axis=dim)
        before = lax.ppermute(last, axis, up)
        after = lax.ppermute(leading, axis, down)
        value = jnp.concatenate([before, value, after], axis=dim)
    return value


def cubic_table():
    columns = jnp.arange(128, dtype=jnp.int32)
    quarter_pos = 3 * columns + 4
    base_tap = quarter_pos // 4
    fraction = (quarter_pos % 4).astype(jnp.float32) / 4.0
    fraction_sq = fraction * fraction
    fraction_cube = fraction_sq * fraction
    weights = [
        (-fraction_cube + 2.0 * fraction_sq - fraction) * 0.5,
        (3.0 * fraction_cube - 5.0 * fraction_sq + 2.0) * 0.5,
        (-3.0 * fraction_cube + 4.0 * fraction_sq + fraction) * 0.5,
        (fraction_cube - fraction_sq) * 0.5,
    ]
    tap_rows = jnp.arange(128, dtype=jnp.int32)[:, None]
    cubic_weights = jnp.zeros((128, 128), jnp.float32)
    for tap_shift, weight in zip(range(-1, 3), weights):
        cubic_weights = cubic_weights + jnp.where(
            tap_rows == (base_tap + tap_shift)[None, :], weight[None, :], 0.0
        )
    return cubic_weights


def block_image(block_echo, block_slope, block_shift, band_start, row_phase, cubic_weights):
    pulses = block_echo.shape[0]
    row_count = band_start.shape[0]
    col_blocks = NCOL // 128
    window_span = 96 * (col_blocks + 1)
    flat_echo = block_echo.reshape(pulses * 2, block_echo.shape[2])
    segments = jax.vmap(
        lambda row_start: lax.dynamic_slice_in_dim(flat_echo, row_start, window_span, axis=1)
    )(band_start)
    leading = segments[..., : 96 * col_blocks].reshape(row_count, pulses * 2, col_blocks, 96)
    trailing = segments[..., 96:].reshape(row_count, pulses * 2, col_blocks, 96)[..., :32]
    windows = jnp.concatenate([leading, trailing], axis=-1)
    windows = (
        jnp.transpose(windows, (0, 2, 1, 3))
        .reshape(row_count, col_blocks, pulses, 2, 128)
        .astype(jnp.float32)
    )
    slopes = block_slope.astype(jnp.float32)
    shifts = block_shift.astype(jnp.float32)
    block_pos = (128 * jnp.arange(col_blocks, dtype=jnp.int32)).astype(jnp.float32)
    angle_grid = (
        shifts[None, None, :] * row_phase[:, None, None]
        + slopes[None, None, :] * block_pos[None, :, None]
    )
    cosine = jnp.cos(angle_grid)[..., None]
    sines = jnp.sin(angle_grid)[..., None]
    real_part = windows[:, :, :, 0]
    imag_part = windows[:, :, :, 1]
    turned_re = real_part * cosine - imag_part * sines
    turned_im = real_part * sines + imag_part * cosine
    turned = (
        jnp.stack([turned_re, turned_im], axis=3)
        .astype(jnp.bfloat16)
        .reshape(row_count * col_blocks, pulses * 256)
    )
    column_pos = jnp.arange(128, dtype=jnp.int32).astype(jnp.float32)
    column_ramp = slopes[:, None] * column_pos[None, :]
    kernel_re = cubic_weights[None] * jnp.cos(column_ramp)[:, None, :]
    kernel_im = cubic_weights[None] * jnp.sin(column_ramp)[:, None, :]
    upper_rows = jnp.concatenate([kernel_re, kernel_im], axis=2)
    bottom = jnp.concatenate([-kernel_im, kernel_re], axis=2)
    kernel = jnp.stack([upper_rows, bottom], axis=1).astype(jnp.bfloat16).reshape(pulses * 256, 256)
    product = jnp.dot(turned, kernel, preferred_element_type=jnp.float32)
    return product.reshape(row_count, col_blocks, 256)


def add_used(
    running, echo_all, slope_all, shift_all, slots, used_count, band_start, row_phase, cubic_weights
):
    slot_count = slots.shape[0]

    def add_pair(pair_index, partial_sum):
        first_slot = slots[2 * pair_index]
        second_slot = slots[jnp.minimum(2 * pair_index + 1, slot_count - 1)]
        second_used = 2 * pair_index + 1 < used_count
        second_echo = jnp.where(second_used, echo_all[second_slot], jnp.zeros_like(echo_all[0]))
        echo_pair = jnp.concatenate([echo_all[first_slot], second_echo], axis=0)
        slope_pair = jnp.concatenate([slope_all[first_slot], slope_all[second_slot]], axis=0)
        shift_pair = jnp.concatenate([shift_all[first_slot], shift_all[second_slot]], axis=0)
        return partial_sum + block_image(
            echo_pair, slope_pair, shift_pair, band_start, row_phase, cubic_weights
        )

    return lax.fori_loop(0, (used_count + 1) // 2, add_pair, running)


def tv_update(field, padded, base_image, row_anchor, col_anchor, grid_rows, grid_cols):
    row_count = field.shape[1]
    col_count = field.shape[2]
    grad_rows = (
        padded[:, 1 : row_count + 2, 0 : col_count + 1]
        - padded[:, 0 : row_count + 1, 0 : col_count + 1]
    )
    grad_cols = (
        padded[:, 0 : row_count + 1, 1 : col_count + 2]
        - padded[:, 0 : row_count + 1, 0 : col_count + 1]
    )
    row_ids = row_anchor - 1 + jnp.arange(row_count + 1, dtype=jnp.int32)
    col_ids = col_anchor - 1 + jnp.arange(col_count + 1, dtype=jnp.int32)
    inside = (row_ids >= 0)[:, None] & (col_ids >= 0)[None, :]
    grad_rows = jnp.where((inside & (row_ids < grid_rows - 1)[:, None])[None], grad_rows, 0.0)
    grad_cols = jnp.where((inside & (col_ids < grid_cols - 1)[None, :])[None], grad_cols, 0.0)
    magnitude = jnp.sqrt(
        jnp.sum(grad_rows * grad_rows + grad_cols * grad_cols, axis=0) + floor_square
    )
    flux_rows = grad_rows / magnitude[None]
    flux_cols = grad_cols / magnitude[None]
    divergence = (
        flux_rows[:, 1:, 1:] - flux_rows[:, :-1, 1:] + flux_cols[:, 1:, 1:] - flux_cols[:, 1:, :-1]
    )
    return field - step_size * (field - base_image - tv_weight * divergence)


def to_image(blocks):
    row_count = blocks.shape[0]
    col_count = blocks.shape[1] * 128
    real_plane = blocks[..., :128].reshape(row_count, col_count)
    imag_plane = blocks[..., 128:].reshape(row_count, col_count)
    return jnp.stack([real_plane, imag_plane])


def body(echoes, pulse_slope, pulse_shift, footprint, band_start, row_phase):
    tile_count = lax.axis_size("tile")
    groups = lax.axis_size("pulse")
    tile_index = lax.axis_index("tile")
    group_index = lax.axis_index("pulse")
    row_count = band_start.shape[0]
    col_blocks = NCOL // 128
    cubic_weights = cubic_table()
    footprints = footprint[0]
    own_list = lax.dynamic_index_in_dim(footprints, tile_index, axis=0, keepdims=False)
    zero_image = jnp.zeros((row_count, col_blocks, 256), jnp.float32)
    piece_echo = lax.all_gather(echoes, "tile", axis=0, tiled=True)
    piece_slope = lax.all_gather(pulse_slope, "tile", axis=0, tiled=True)
    piece_shift = lax.all_gather(pulse_shift, "tile", axis=0, tiled=True)
    piece_count = piece_echo.shape[0]
    positions = jnp.arange(piece_count, dtype=jnp.int32)
    is_used = jnp.any(positions[:, None] == own_list[None, :], axis=1)
    ordering = jnp.argsort(jnp.where(is_used, 0, piece_count) + positions)
    used_total = jnp.sum(is_used.astype(jnp.int32))
    partial_image = add_used(
        zero_image,
        piece_echo,
        piece_slope,
        piece_shift,
        ordering,
        used_total,
        band_start,
        row_phase,
        cubic_weights,
    )
    normalize = float(PB * tile_count * groups) ** (-0.5)
    grid_rows = tile_count * row_count
    row_anchor = tile_index * row_count
    whole = lax.psum(partial_image, "pulse")
    base_image = to_image(whole) * normalize
    field = base_image
    for iteration in range(ITERS):
        padded = padded_2(field, (("tile", 1),), 1)
        padded = jnp.pad(padded, ((0, 0), (0, 0), (1, 1)))
        field = tv_update(field, padded, base_image, row_anchor, 0, grid_rows, NCOL)
    share_width = NCOL // groups
    return lax.dynamic_slice_in_dim(field, group_index * share_width, share_width, axis=2)


def solution(mesh):
    in_specs = (
        P(("pulse", "tile"), None, None, None),
        P(("pulse", "tile"), None),
        P(("pulse", "tile"), None),
        P("pulse", None, None),
        P("tile"),
        P("tile"),
    )
    out_specs = P(None, "tile", "pulse")
    return jax.shard_map(body, mesh=mesh, in_specs=in_specs, out_specs=out_specs, check_vma=False)
```

profile of v0, /device:TPU:64, one launch (start us, length us, event | category | flops | bytes accessed | tf_op | source)
XLA Modules:
  0.0 1211.1 jit_solution(6912679305393457067)
XLA Ops:
  8.7 2.0 sort.17
  10.7 40.3 %all-gather = bf16[32,2,2]{2,1,0:T(2,128)(2,1)S(1)} all-gather(bf16[1,2,2]{2,1,0:T(2,128)(2,1)} %bitcast.74), channel_id=1, replica_groups=mesh['pulse'=8,'tile'=32] {'tile'}, dimensions={0}, use_global_device_ids=true | all-gather | bytes 264 | tf_op jit(solution)/shard_map/all_gather | solution.py:163
  51.0 37.3 %all-gather.1 = bf16[32,2,2]{2,1,0:T(2,128)(2,1)S(1)} all-gather(bf16[1,2,2]{2,1,0:T(2,128)(2,1)} %bitcast.75), channel_id=1, replica_groups=mesh['pulse'=8,'tile'=32] {'tile'}, dimensions={0}, use_global_device_ids=true | all-gather | bytes 264 | tf_op jit(solution)/shard_map/all_gather | solution.py:162
  88.4 20.5 %all-gather.4.cloned.1.call-done = bf16[64,2,2,16384]{3,2,1,0:T(2,128)(2,1)} async-done(((bf16[2,2,2,16384]{3,2,1,0:T(2,128)(2,1)}), bf16[64,2,2,16384]{3,2,1,0:T(2,128)(2,1)}) %all-gather.4.cloned.1.call-update) | async-done | bytes 8388624 | tf_op jit(solution)/shard_map/all_gather | solution.py:161
  109.1 437.2 %while.17 = (s32[]{:T(128)}, f32[32,32,256]{2,1,0:T(8,128)S(1)}, s32[]{:T(128)}, s32[64]{0:T(128)S(1)}, bf16[64,2,2,16384]{3,2,1,0:T(2,128)(2,1)}, /*index=5*/s3...) while((s32[]{:T(128)}, f32[32,32,256]{2,1,0:T(8,128)S(1)}, ...), condition=%wide.region_4.5_spmd.clone.clone, body=%wide.region_3.4_spmd.clone.clone.sunk | while | flops 548656192 | bytes 41472712 | solution.py:112
  113.8 1.2 dynamic-slice_bitcast_fusion.2
  115.5 39.0 %while.18 = (s32[]{:T(128)}, bf16[8,16384]{1,0:T(8,128)(2,1)S(1)}, s32[32,2]{0,1:T(2,128)S(1)}, bf16[32,8,3168]{2,1,0:T(8,128)(2,1)S(1)}, s32[]{:T(128)}) while((s32[]{:T(128)}, bf16[8,16384]{1,0:T(8,128)(2,1)S(1)}, s32[32,2]{0,1:T(2,128)S(1)}, bf16[32,8,3168]{2,1,0:T(8,128)(2,1)S(1)}, s32[]{:T(128)}) %tuple.94), condition=%wide.while_cond, body=%wide.while_body.sunk | while | flops 2 | bytes 102497 | solution.py:56
  154.5 2.4 fusion.59
  157.0 3.6 reshape.426
  160.6 4.5 reshape.427
  165.1 2.6 maximum_convert_fusion.6
  169.0 1.4 subtract_convert_fusion.2
  176.3 1.2 dynamic-slice_bitcast_fusion.2
  178.0 39.0 %while.18 = (s32[]{:T(128)}, bf16[8,16384]{1,0:T(8,128)(2,1)S(1)}, s32[32,2]{0,1:T(2,128)S(1)}, bf16[32,8,3168]{2,1,0:T(8,128)(2,1)S(1)}, s32[]{:T(128)}) while((s32[]{:T(128)}, bf16[8,16384]{1,0:T(8,128)(2,1)S(1)}, s32[32,2]{0,1:T(2,128)S(1)}, bf16[32,8,3168]{2,1,0:T(8,128)(2,1)S(1)}, s32[]{:T(128)}) %tuple.94), condition=%wide.while_cond, body=%wide.while_body.sunk | while | flops 2 | bytes 102497 | solution.py:56
  217.0 2.4 fusion.59
  219.4 3.6 reshape.426
  223.0 4.5 reshape.427
  227.6 2.6 maximum_convert_fusion.6
  231.5 1.4 subtract_convert_fusion.2
  238.7 1.2 dynamic-slice_bitcast_fusion.2
  240.4 39.0 %while.18 = (s32[]{:T(128)}, bf16[8,16384]{1,0:T(8,128)(2,1)S(1)}, s32[32,2]{0,1:T(2,128)S(1)}, bf16[32,8,3168]{2,1,0:T(8,128)(2,1)S(1)}, s32[]{:T(128)}) while((s32[]{:T(128)}, bf16[8,16384]{1,0:T(8,128)(2,1)S(1)}, s32[32,2]{0,1:T(2,128)S(1)}, bf16[32,8,3168]{2,1,0:T(8,128)(2,1)S(1)}, s32[]{:T(128)}) %tuple.94), condition=%wide.while_cond, body=%wide.while_body.sunk | while | flops 2 | bytes 102497 | solution.py:56
  279.4 2.4 fusion.59
  281.9 3.6 reshape.426
  285.5 4.5 reshape.427
  290.0 2.6 maximum_convert_fusion.6
  294.0 1.4 subtract_convert_fusion.2
  301.2 1.2 dynamic-slice_bitcast_fusion.2
  302.9 39.0 %while.18 = (s32[]{:T(128)}, bf16[8,16384]{1,0:T(8,128)(2,1)S(1)}, s32[32,2]{0,1:T(2,128)S(1)}, bf16[32,8,3168]{2,1,0:T(8,128)(2,1)S(1)}, s32[]{:T(128)}) while((s32[]{:T(128)}, bf16[8,16384]{1,0:T(8,128)(2,1)S(1)}, s32[32,2]{0,1:T(2,128)S(1)}, bf16[32,8,3168]{2,1,0:T(8,128)(2,1)S(1)}, s32[]{:T(128)}) %tuple.94), condition=%wide.while_cond, body=%wide.while_body.sunk | while | flops 2 | bytes 102497 | solution.py:56
  341.9 2.4 fusion.59
  344.3 3.6 reshape.426
  347.9 4.5 reshape.427
  352.5 2.6 maximum_convert_fusion.6
  356.4 1.4 subtract_convert_fusion.2
  363.6 1.2 dynamic-slice_bitcast_fusion.2
  365.3 39.0 %while.18 = (s32[]{:T(128)}, bf16[8,16384]{1,0:T(8,128)(2,1)S(1)}, s32[32,2]{0,1:T(2,128)S(1)}, bf16[32,8,3168]{2,1,0:T(8,128)(2,1)S(1)}, s32[]{:T(128)}) while((s32[]{:T(128)}, bf16[8,16384]{1,0:T(8,128)(2,1)S(1)}, s32[32,2]{0,1:T(2,128)S(1)}, bf16[32,8,3168]{2,1,0:T(8,128)(2,1)S(1)}, s32[]{:T(128)}) %tuple.94), condition=%wide.while_cond, body=%wide.while_body.sunk | while | flops 2 | bytes 102497 | solution.py:56
  404.4 2.4 fusion.59
  406.8 3.6 reshape.426
  410.4 4.5 reshape.427
  414.9 2.6 maximum_convert_fusion.6
  418.9 1.4 subtract_convert_fusion.2
  426.1 1.2 dynamic-slice_bitcast_fusion.2
  427.8 39.0 %while.18 = (s32[]{:T(128)}, bf16[8,16384]{1,0:T(8,128)(2,1)S(1)}, s32[32,2]{0,1:T(2,128)S(1)}, bf16[32,8,3168]{2,1,0:T(8,128)(2,1)S(1)}, s32[]{:T(128)}) while((s32[]{:T(128)}, bf16[8,16384]{1,0:T(8,128)(2,1)S(1)}, s32[32,2]{0,1:T(2,128)S(1)}, bf16[32,8,3168]{2,1,0:T(8,128)(2,1)S(1)}, s32[]{:T(128)}) %tuple.94), condition=%wide.while_cond, body=%wide.while_body.sunk | while | flops 2 | bytes 102497 | solution.py:56
  466.8 2.4 fusion.59
  469.2 3.6 reshape.426
  472.8 4.5 reshape.427
  477.4 2.6 maximum_convert_fusion.6
  481.3 1.4 subtract_convert_fusion.2
  488.5 1.2 dynamic-slice_bitcast_fusion.2
  490.2 39.0 %while.18 = (s32[]{:T(128)}, bf16[8,16384]{1,0:T(8,128)(2,1)S(1)}, s32[32,2]{0,1:T(2,128)S(1)}, bf16[32,8,3168]{2,1,0:T(8,128)(2,1)S(1)}, s32[]{:T(128)}) while((s32[]{:T(128)}, bf16[8,16384]{1,0:T(8,128)(2,1)S(1)}, s32[32,2]{0,1:T(2,128)S(1)}, bf16[32,8,3168]{2,1,0:T(8,128)(2,1)S(1)}, s32[]{:T(128)}) %tuple.94), condition=%wide.while_cond, body=%wide.while_body.sunk | while | flops 2 | bytes 102497 | solution.py:56
  529.3 2.4 fusion.59
  531.7 3.6 reshape.426
  535.3 4.5 reshape.427
  539.8 2.6 maximum_convert_fusion.6
  543.8 1.4 subtract_convert_fusion.2
  546.3 1.0 copy-done.1
  547.3 627.9 %all-reduce.5.cloned.1.call-done = f32[32,32,256]{2,1,0:T(8,128)} async-done(((f32[32,32,256]{2,1,0:T(8,128)}), f32[32,32,256]{2,1,0:T(8,128)}) %all-reduce.5.cloned.1.call-update) | async-done | bytes 1048592 | tf_op jit(solution)/shard_map/psum | solution.py:183
  1175.2 1.3 fusion.50
  1176.8 3.5 collective-permute-start
  1180.3 2.4 collective-permute-start.1
  1183.0 3.9 collective-permute-done.1
  1188.8 0.9 fusion.29
  1189.7 5.1 collective-permute-start.2
  1194.9 2.1 collective-permute-start.3
  1197.0 3.7 collective-permute-done.3
  (853 shorter events, 300.5 us)
Async XLA Ops:
  6.5 0.8 copy-start
  6.5 102.5 %copy-start.3 = (s32[32]{0:T(128)S(1)}, s32[32]{0:T(128)}, u32[]{:S(2)}) copy-start(s32[32]{0:T(128)} %param.12) | copy-start | bytes 388
  6.5 102.5 %copy-start.2 = (f32[32]{0:T(128)S(1)}, f32[32]{0:T(128)}, u32[]{:S(2)}) copy-start(f32[32]{0:T(128)} %param.13) | copy-start | bytes 388
  6.5 102.4 %all-gather.4.cloned.1.call-start = ((), (), s32[]{:S(2)}) async-start(), calls=%async_computation | async-start | bytes 8650752 | tf_op jit(solution)/shard_map/all_gather | solution.py:161
  7.3 1167.9 %all-reduce.5.cloned.1.call-start = ((), (), s32[]{:S(2)}) async-start(), calls=%async_computation.1 | async-start | bytes 2097152 | tf_op jit(solution)/shard_map/psum | solution.py:183
  546.3 1.0 copy-start.1
  1176.8 6.1 collective-permute-start
  1180.3 6.6 collective-permute-start.1
  1189.7 7.3 collective-permute-start.2
  1194.9 5.8 collective-permute-start.3
Sparse Core Ops, SparseCore 0:
  9.9 98.9 all-gather.3
  547.4 627.7 all-reduce.4
where the time goes:
time: 1220 us; the launch traced here: 1210 us
  waiting for transfers between devices  657 us (54%)
  local copies, waits for them, and re-layouts  356 us (29%)
  blocking collectives  77.7 us (6%)
  other arithmetic  54.3 us (4%)
  loops' own time  33.9 us (3%)
  between operations  14.2 us (1%)
  starting transfers between devices  13.1 us (1%)
    psum x1, waiting for transfers between devices, body(): whole = lax.psum(partial_image, 'pulse')  628 us
    gather x672, local copies, waits for them, and re-layouts  269 us
    all_gather x1, blocking collectives, body(): piece_shift = lax.all_gather(pulse_shift, 'tile', axis=0, tiled=True)  40.3 us
    all_gather x1, blocking collectives, body(): piece_slope = lax.all_gather(pulse_slope, 'tile', axis=0, tiled=True)  37.3 us
    reshape x7, local copies, waits for them, and re-layouts, block_image(): segments[..., :96 * col_blocks]  31.8 us
    another operation x1, loops' own time, add_used(): return lax.fori_loop(0, (used_count + 1) // 2, add_pair, running)  29.9 us
    reshape x7, local copies, waits for them, and re-layouts, block_image(): segments[..., 96:].reshape(row_count, pulses * 2, col_blocks, 96)[..., :32]  25.1 us
  transfers between devices with their start and end apart: 6, of which 4 were waited for; matrix products, arithmetic and copies ran while one was open for 0% of the time, Pallas kernels for 0%

commit v1 on v0

--- a/solution.py
+++ b/solution.py
@@ -159,8 +159,13 @@
     own_list = lax.dynamic_index_in_dim(footprints, tile_index, axis=0, keepdims=False)
     zero_image = jnp.zeros((row_count, col_blocks, 256), jnp.float32)
     piece_echo = lax.all_gather(echoes, "tile", axis=0, tiled=True)
-    piece_slope = lax.all_gather(pulse_slope, "tile", axis=0, tiled=True)
-    piece_shift = lax.all_gather(pulse_shift, "tile", axis=0, tiled=True)
+    piece_slope, piece_shift = jnp.split(
+        lax.all_gather(
+            jnp.concatenate([pulse_slope, pulse_shift], axis=1), "tile", axis=0, tiled=True
+        ),
+        [pulse_slope.shape[1]],
+        axis=1,
+    )
     piece_count = piece_echo.shape[0]
     positions = jnp.arange(piece_count, dtype=jnp.int32)
     is_used = jnp.any(positions[:, None] == own_list[None, :], axis=1)

time: 1220 us -> 1290 us (1.057)
  waiting for transfers between devices: 657 us -> 734 us
  blocking collectives: 77.7 us -> 40.3 us
  local copies, waits for them, and re-layouts: 356 us -> 386 us
    psum x1, waiting for transfers between devices: 628 us -> 669 us  [body(): whole = lax.psum(partial_image, 'pulse')]
    all_gather x2 -> x1, blocking collectives: 77.7 us -> 40.3 us  [body(): lax.all_gather(jnp.concatenate([pulse_slope, pulse_shift], axis=1), 'tile...]
    all_gather x1, waiting for transfers between devices: 20.5 us -> 57 us  [body(): piece_echo = lax.all_gather(echoes, 'tile', axis=0, tiled=True)]
    gather x672, local copies, waits for them, and re-layouts: 269 us -> 299 us
where the time goes in v1:
time: 1290 us; the launch traced here: 1280 us
  waiting for transfers between devices  734 us (57%)
  local copies, waits for them, and re-layouts  386 us (30%)
  other arithmetic  55.1 us (4%)
  blocking collectives  40.3 us (3%)
  loops' own time  35.9 us (3%)
  between operations  14.3 us (1%)
  starting transfers between devices  13.1 us (1%)
    psum x1, waiting for transfers between devices, body(): whole = lax.psum(partial_image, 'pulse')  669 us
    gather x672, local copies, waits for them, and re-layouts  299 us
    all_gather x1, waiting for transfers between devices, body(): piece_echo = lax.all_gather(echoes, 'tile', axis=0, tiled=True)  57 us
    all_gather x1, blocking collectives, body(): lax.all_gather(jnp.concatenate([pulse_slope, pulse_shift], axis=1), 'tile...  40.3 us
    another operation x1, loops' own time, add_used(): return lax.fori_loop(0, (used_count + 1) // 2, add_pair, running)  31.9 us
    reshape x7, local copies, waits for them, and re-layouts, block_image(): segments[..., :96 * col_blocks]  31.8 us
  transfers between devices with their start and end apart: 6, of which 4 were waited for; matrix products, arithmetic and copies ran while one was open for 0% of the time, Pallas kernels for 0%

profile of v1, /device:TPU:64, one launch (start us, length us, event | category | flops | bytes accessed | tf_op | source)
XLA Modules:
  0.0 1284.4 jit_solution(10820963235437287485)
XLA Ops:
  8.7 2.0 sort.17
  10.7 0.7 maximum_bitcast_fusion.4
  11.5 40.3 %all-gather = bf16[32,2,4]{2,1,0:T(2,128)(2,1)S(1)} all-gather(bf16[1,2,4]{2,1,0:T(2,128)(2,1)S(1)} %maximum_bitcast_fusion.4), channel_id=1, replica_groups=mesh['pulse'=8,'tile'=32] {'tile'}, dimensions={0}, use_global_device_ids=true | all-gather | bytes 528 | tf_op jit(solution)/shard_map/all_gather | solution.py:163
  52.0 57.0 %all-gather.3.cloned.1.call-done = bf16[64,2,2,16384]{3,2,1,0:T(2,128)(2,1)} async-done(((bf16[2,2,2,16384]{3,2,1,0:T(2,128)(2,1)}), bf16[64,2,2,16384]{3,2,1,0:T(2,128)(2,1)}) %all-gather.3.cloned.1.call-update) | async-done | bytes 8388624 | tf_op jit(solution)/shard_map/all_gather | solution.py:161
  109.1 469.2 %while.17 = (s32[]{:T(128)}, f32[32,32,256]{2,1,0:T(8,128)S(1)}, s32[]{:T(128)}, s32[64]{0:T(128)S(1)}, bf16[64,2,2,16384]{3,2,1,0:T(2,128)(2,1)}, /*index=5*/s3...) while((s32[]{:T(128)}, f32[32,32,256]{2,1,0:T(8,128)S(1)}, ...), condition=%wide.region_4.5_spmd.clone.clone, body=%wide.region_3.4_spmd.clone.clone.sunk | while | flops 548656192 | bytes 41472712 | solution.py:112
  114.2 1.2 dynamic-slice_bitcast_fusion.2
  115.8 43.3 %while.18 = (s32[]{:T(128)}, bf16[8,16384]{1,0:T(8,128)(2,1)S(1)}, s32[32,2]{0,1:T(2,128)S(1)}, bf16[32,8,3168]{2,1,0:T(8,128)(2,1)S(1)}, s32[]{:T(128)}) while((s32[]{:T(128)}, bf16[8,16384]{1,0:T(8,128)(2,1)S(1)}, s32[32,2]{0,1:T(2,128)S(1)}, bf16[32,8,3168]{2,1,0:T(8,128)(2,1)S(1)}, s32[]{:T(128)}) %tuple.90), condition=%wide.while_cond, body=%wide.while_body.sunk | while | flops 2 | bytes 102497 | solution.py:56
  159.1 2.4 fusion.60
  161.6 3.6 reshape.424
  165.2 4.5 reshape.425
  169.7 2.6 maximum_convert_fusion.6
  173.6 1.4 subtract_convert_fusion.2
  181.2 1.2 dynamic-slice_bitcast_fusion.2
  182.9 43.3 %while.18 = (s32[]{:T(128)}, bf16[8,16384]{1,0:T(8,128)(2,1)S(1)}, s32[32,2]{0,1:T(2,128)S(1)}, bf16[32,8,3168]{2,1,0:T(8,128)(2,1)S(1)}, s32[]{:T(128)}) while((s32[]{:T(128)}, bf16[8,16384]{1,0:T(8,128)(2,1)S(1)}, s32[32,2]{0,1:T(2,128)S(1)}, bf16[32,8,3168]{2,1,0:T(8,128)(2,1)S(1)}, s32[]{:T(128)}) %tuple.90), condition=%wide.while_cond, body=%wide.while_body.sunk | while | flops 2 | bytes 102497 | solution.py:56
  226.2 2.4 fusion.60
  228.6 3.6 reshape.424
  232.2 4.5 reshape.425
  236.7 2.6 maximum_convert_fusion.6
  240.7 1.4 subtract_convert_fusion.2
  248.2 1.2 dynamic-slice_bitcast_fusion.2
  249.9 43.3 %while.18 = (s32[]{:T(128)}, bf16[8,16384]{1,0:T(8,128)(2,1)S(1)}, s32[32,2]{0,1:T(2,128)S(1)}, bf16[32,8,3168]{2,1,0:T(8,128)(2,1)S(1)}, s32[]{:T(128)}) while((s32[]{:T(128)}, bf16[8,16384]{1,0:T(8,128)(2,1)S(1)}, s32[32,2]{0,1:T(2,128)S(1)}, bf16[32,8,3168]{2,1,0:T(8,128)(2,1)S(1)}, s32[]{:T(128)}) %tuple.90), condition=%wide.while_cond, body=%wide.while_body.sunk | while | flops 2 | bytes 102497 | solution.py:56
  293.2 2.4 fusion.60
  295.6 3.6 reshape.424
  299.2 4.5 reshape.425
  303.8 2.6 maximum_convert_fusion.6
  307.7 1.4 subtract_convert_fusion.2
  315.2 1.2 dynamic-slice_bitcast_fusion.2
  316.9 43.3 %while.18 = (s32[]{:T(128)}, bf16[8,16384]{1,0:T(8,128)(2,1)S(1)}, s32[32,2]{0,1:T(2,128)S(1)}, bf16[32,8,3168]{2,1,0:T(8,128)(2,1)S(1)}, s32[]{:T(128)}) while((s32[]{:T(128)}, bf16[8,16384]{1,0:T(8,128)(2,1)S(1)}, s32[32,2]{0,1:T(2,128)S(1)}, bf16[32,8,3168]{2,1,0:T(8,128)(2,1)S(1)}, s32[]{:T(128)}) %tuple.90), condition=%wide.while_cond, body=%wide.while_body.sunk | while | flops 2 | bytes 102497 | solution.py:56
  360.2 2.4 fusion.60
  362.7 3.6 reshape.424
  366.2 4.5 reshape.425
  370.8 2.6 maximum_convert_fusion.6
  374.7 1.4 subtract_convert_fusion.2
  382.3 1.2 dynamic-slice_bitcast_fusion.2
  383.9 43.3 %while.18 = (s32[]{:T(128)}, bf16[8,16384]{1,0:T(8,128)(2,1)S(1)}, s32[32,2]{0,1:T(2,128)S(1)}, bf16[32,8,3168]{2,1,0:T(8,128)(2,1)S(1)}, s32[]{:T(128)}) while((s32[]{:T(128)}, bf16[8,16384]{1,0:T(8,128)(2,1)S(1)}, s32[32,2]{0,1:T(2,128)S(1)}, bf16[32,8,3168]{2,1,0:T(8,128)(2,1)S(1)}, s32[]{:T(128)}) %tuple.90), condition=%wide.while_cond, body=%wide.while_body.sunk | while | flops 2 | bytes 102497 | solution.py:56
  427.3 2.4 fusion.60
  429.7 3.6 reshape.424
  433.3 4.5 reshape.425
  437.8 2.6 maximum_convert_fusion.6
  441.7 1.4 subtract_convert_fusion.2
  449.3 1.2 dynamic-slice_bitcast_fusion.2
  451.0 43.3 %while.18 = (s32[]{:T(128)}, bf16[8,16384]{1,0:T(8,128)(2,1)S(1)}, s32[32,2]{0,1:T(2,128)S(1)}, bf16[32,8,3168]{2,1,0:T(8,128)(2,1)S(1)}, s32[]{:T(128)}) while((s32[]{:T(128)}, bf16[8,16384]{1,0:T(8,128)(2,1)S(1)}, s32[32,2]{0,1:T(2,128)S(1)}, bf16[32,8,3168]{2,1,0:T(8,128)(2,1)S(1)}, s32[]{:T(128)}) %tuple.90), condition=%wide.while_cond, body=%wide.while_body.sunk | while | flops 2 | bytes 102497 | solution.py:56
  494.3 2.4 fusion.60
  496.7 3.6 reshape.424
  500.3 4.5 reshape.425
  504.9 2.6 maximum_convert_fusion.6
  508.8 1.4 subtract_convert_fusion.2
  516.3 1.2 dynamic-slice_bitcast_fusion.2
  518.0 43.3 %while.18 = (s32[]{:T(128)}, bf16[8,16384]{1,0:T(8,128)(2,1)S(1)}, s32[32,2]{0,1:T(2,128)S(1)}, bf16[32,8,3168]{2,1,0:T(8,128)(2,1)S(1)}, s32[]{:T(128)}) while((s32[]{:T(128)}, bf16[8,16384]{1,0:T(8,128)(2,1)S(1)}, s32[32,2]{0,1:T(2,128)S(1)}, bf16[32,8,3168]{2,1,0:T(8,128)(2,1)S(1)}, s32[]{:T(128)}) %tuple.90), condition=%wide.while_cond, body=%wide.while_body.sunk | while | flops 2 | bytes 102497 | solution.py:56
  561.3 2.4 fusion.60
  563.7 3.6 reshape.424
  567.3 4.5 reshape.425
  571.9 2.6 maximum_convert_fusion.6
  575.8 1.4 subtract_convert_fusion.2
  578.3 1.0 copy-done.1
  579.3 669.1 %all-reduce.5.cloned.1.call-done = f32[32,32,256]{2,1,0:T(8,128)} async-done(((f32[32,32,256]{2,1,0:T(8,128)}), f32[32,32,256]{2,1,0:T(8,128)}) %all-reduce.5.cloned.1.call-update) | async-done | bytes 1048592 | tf_op jit(solution)/shard_map/psum | solution.py:188
  1248.4 1.3 fusion.50
  1250.1 3.5 collective-permute-start
  1253.6 2.4 collective-permute-start.1
  1256.2 3.9 collective-permute-done.1
  1262.0 0.9 fusion.29
  1263.0 5.1 collective-permute-start.2
  1268.1 2.1 collective-permute-start.3
  1270.2 3.7 collective-permute-done.3
  (854 shorter events, 330.7 us)
Async XLA Ops:
  6.5 0.8 copy-start
  6.5 102.5 %copy-start.3 = (s32[32]{0:T(128)S(1)}, s32[32]{0:T(128)}, u32[]{:S(2)}) copy-start(s32[32]{0:T(128)} %param.12) | copy-start | bytes 388
  6.5 102.5 %copy-start.2 = (f32[32]{0:T(128)S(1)}, f32[32]{0:T(128)}, u32[]{:S(2)}) copy-start(f32[32]{0:T(128)} %param.13) | copy-start | bytes 388
  6.5 102.4 %all-gather.3.cloned.1.call-start = ((), (), s32[]{:S(2)}) async-start(), calls=%async_computation | async-start | bytes 8650752 | tf_op jit(solution)/shard_map/all_gather | solution.py:161
  7.3 1241.2 %all-reduce.5.cloned.1.call-start = ((), (), s32[]{:S(2)}) async-start(), calls=%async_computation.1 | async-start | bytes 2097152 | tf_op jit(solution)/shard_map/psum | solution.py:188
  578.3 1.0 copy-start.1
  1250.1 6.1 collective-permute-start
  1253.6 6.6 collective-permute-start.1
  1263.0 7.3 collective-permute-start.2
  1268.1 5.8 collective-permute-start.3
Sparse Core Ops, SparseCore 0:
  9.9 98.9 all-gather.2
  579.4 668.9 all-reduce.4
